TPU v7x, 32 devices: a whole 2x2x4 slice. The times are simulated.
32 devices in a mesh: video: 2 (over y), block: 4 (over z), band: 2 (over x), chan: 2 (over core).
Axes of the slice: x: 2, y: 2, z: 4, core: 2. Of those that a mesh axis runs over, the one named last changes fastest.
Arguments:
- latents: bfloat16 [32, 2, 1664], P(('video', 'block'), 'band'), parts along dimension 0, may hold values from -60 to 60
- frame_counts: int32 [8], P('video'), parts along dimension 0, may hold values from 1 to 4, 8 in all
- w_in: bfloat16 [3, 3, 3, 16, 384], replicated, may hold values from -0.3125 to 0.3125
- gain_in: float32 [384], replicated, may hold values from 0.1 to 1.9
- shift_in: float32 [384], replicated, may hold values from -3 to 3
- w_mid: bfloat16 [3, 3, 3, 384, 384], P(None, None, None, None, 'chan'), may hold values from -0.0625 to 0.0625
- gain_out: float32 [384], P('chan'), may hold values from 0.1 to 1.9
- shift_out: float32 [384], P('chan'), may hold values from -3 to 3
Outputs:
- decoded: bfloat16 [32, 2, 104, 384], P(('video', 'block'), 'band', None, 'chan'), parts along dimension 0
There are 2 independent parts, one for each index of `video`. A program takes and returns all parts, laid end to end along the dimension named above; an argument that names none is the same for every part. Nothing has to cross between parts.
Inputs may be any that keep to these rules, and one draw needn't show every extreme that they name: `frame_counts`: entry k is the number of consecutive latent frames that device k of the frame axis holds; the entries sum to 8.
All inputs are finite; a program needn't handle non-finite values.
Results may differ from a plain program's by a relative error of at most 0.013.
Values may be sent and summed in bfloat16 or wider, within the bound.
No kernel may reach another device: no remote copies, remote signals or barrier semaphores. Data moves between devices by JAX's collectives and lax.ppermute only.
A program may use at most 64 MiB of HBM per device.

v0:
```python
import jax
import jax.numpy as jnp
from jax import lax
from jax.sharding import PartitionSpec as P

LAT = 16
C = 384
GROUPS = 32
EPSILON = 1e-06


def with_halo(cells, sides, width):
    for axis, dim in sides:
        count = lax.axis_size(axis)
        ends = count - 1
        head = lax.slice_in_dim(cells, 0, width, axis=dim)
        tail = lax.slice_in_dim(cells, cells.shape[dim] - width, cells.shape[dim], axis=dim)
        cells = jnp.concatenate(
            [
                lax.ppermute(tail, axis, [(i, (i + 1) % count) for i in range(ends)]),
                cells,
                lax.ppermute(head, axis, [((i + 1) % count, i) for i in range(ends)]),
            ],
            axis=dim,
        )
    return cells


def count_for(frame_counts, position):
    places = jnp.arange(frame_counts.shape[0], dtype=jnp.int32)
    return jnp.sum(jnp.where(places == position, frame_counts, 0))


def start_for(frame_counts, position):
    places = jnp.arange(frame_counts.shape[0], dtype=jnp.int32)
    return jnp.sum(jnp.where(places < position, frame_counts, 0))


def rows_beside(values):
    return with_halo(values, (("band", 1),), 1)


def group_silu(values, norm_gain, norm_shift):
    in_frames, band_rows, columns, local_width = values.shape
    group_width = C // GROUPS
    local_groups = local_width // group_width
    grouped = values.reshape(in_frames, band_rows * columns, local_groups, group_width)
    group_total, squares = lax.psum(
        (jnp.sum(grouped, axis=(1, 3)), jnp.sum(grouped * grouped, axis=(1, 3))), "band"
    )
    total = float(lax.axis_size("band") * band_rows * columns * group_width)
    group_mean = group_total / total
    variance = squares / total - group_mean * group_mean
    inverse = lax.rsqrt(variance + EPSILON)
    normed = (grouped - group_mean[:, None, :, None]) * inverse[:, None, :, None]
    normed = normed.reshape(values.shape)
    return jax.nn.silu(normed * norm_gain + norm_shift)


def latent_conv(extended, kernel):
    steps_in, rows_padded, flat_width = extended.shape
    lat_width = kernel.shape[3]
    out_width = kernel.shape[4]
    columns = flat_width // lat_width
    out_frames = steps_in - 2
    band_rows = rows_padded - 2
    latent_grid = extended.reshape(steps_in, rows_padded, columns, lat_width)
    latent_grid = jnp.pad(latent_grid, ((0, 0), (0, 0), (1, 1), (0, 0)))
    patches = []
    for step_t in range(3):
        for step_y in range(3):
            for step_x in range(3):
                patches.append(
                    latent_grid[
                        step_t : step_t + out_frames,
                        step_y : step_y + band_rows,
                        step_x : step_x + columns,
                        :,
                    ]
                )
    stacked = jnp.concatenate(patches, axis=-1).reshape(-1, 27 * lat_width)
    result = jnp.dot(
        stacked, kernel.reshape(27 * lat_width, out_width), preferred_element_type=jnp.float32
    )
    return result.reshape(out_frames, band_rows, columns, out_width)


def weighted_taps(padded, kernel):
    in_frames, rows_padded, cols_padded, in_width = padded.shape
    out_frames = in_frames - 2
    band_rows = rows_padded - 2
    columns = cols_padded - 2
    out_width = kernel.shape[4]
    accumulate = jnp.zeros((out_frames * band_rows * columns, out_width), jnp.float32)
    for step_t in range(3):
        for step_y in range(3):
            patches = [
                padded[
                    step_t : step_t + out_frames,
                    step_y : step_y + band_rows,
                    step_x : step_x + columns,
                    :,
                ]
                for step_x in range(3)
            ]
            stacked = jnp.concatenate(patches, axis=-1).reshape(-1, 3 * in_width)
            accumulate = accumulate + jnp.dot(
                stacked,
                kernel[step_t, step_y].reshape(3 * in_width, out_width),
                preferred_element_type=jnp.float32,
            )
    return accumulate.reshape(out_frames, band_rows, columns, out_width)


def middle_section(act_extended, w_mid, gain_out, shift_out):
    padded = jnp.pad(rows_beside(act_extended), ((0, 0), (0, 0), (1, 1), (0, 0)))
    second_conv = weighted_taps(lax.all_gather(padded, "chan", axis=3, tiled=True), w_mid)
    second_conv = second_conv.astype(jnp.bfloat16)
    return group_silu(second_conv.astype(jnp.float32), gain_out, shift_out).astype(jnp.bfloat16)


def shards(latents, frame_counts, w_in, gain_in, shift_in, w_mid, gain_out, shift_out):
    frames, band_rows, flat_width = latents.shape
    columns = flat_width // LAT
    half_width = w_mid.shape[4]
    position = lax.axis_index("block")
    live_count = count_for(frame_counts, position)
    offset = lax.axis_index("chan") * half_width
    front_kernel = lax.dynamic_slice_in_dim(w_in, offset, half_width, 4)
    front_gain = lax.dynamic_slice_in_dim(gain_in, offset, half_width, 0)
    front_shift = lax.dynamic_slice_in_dim(shift_in, offset, half_width, 0)
    share = frames // 2
    all_slots = lax.all_gather(latents, "block", axis=0, tiled=True)
    run_ends = jnp.cumsum(frame_counts)
    run_starts = run_ends - frame_counts
    first_frame = position * share - 4
    wanted = first_frame + jnp.arange(share + 4, dtype=jnp.int32)
    owners = jnp.sum((wanted[:, None] >= run_ends[None, :]).astype(jnp.int32), axis=1)
    slot_ids = owners * frames + wanted - jnp.take(run_starts, owners)
    slot_ids = jnp.clip(slot_ids, 0, all_slots.shape[0] - 1)
    picked = jnp.take(all_slots, slot_ids, axis=0)
    latent_extended = jnp.where((wanted >= 0)[:, None, None], picked, jnp.zeros_like(picked))
    first_conv = latent_conv(rows_beside(latent_extended), front_kernel).astype(jnp.bfloat16)
    activated = group_silu(first_conv.astype(jnp.float32), front_gain, front_shift).astype(
        jnp.bfloat16
    )
    act_ids = first_frame + 2 + jnp.arange(share + 2, dtype=jnp.int32)
    act_extended = jnp.where(
        (act_ids >= 0)[:, None, None, None], activated, jnp.zeros_like(activated)
    )
    even_norm = middle_section(act_extended, w_mid, gain_out, shift_out)
    my_start = start_for(frame_counts, position)
    slot_places = jnp.arange(frames, dtype=jnp.int32)
    slot_frames = my_start + slot_places
    slot_alive = slot_places < live_count
    initial = jnp.zeros((frames, band_rows, columns, half_width), jnp.bfloat16)
    piece = lax.all_gather(even_norm, "block", axis=0, tiled=True)
    valid = (slot_frames >= 0) & (slot_frames < piece.shape[0]) & slot_alive
    took = jnp.take(piece, jnp.clip(slot_frames, 0, piece.shape[0] - 1), axis=0)
    return jnp.where(valid[:, None, None, None], took, initial)


def solution(mesh):
    return jax.shard_map(
        shards,
        mesh=mesh,
        in_specs=(
            P(("video", "block"), "band", None),
            P("video"),
            P(),
            P(),
            P(),
            P(None, None, None, None, "chan"),
            P("chan"),
            P("chan"),
        ),
        out_specs=P(("video", "block"), "band", None, "chan"),
        check_vma=False,
    )
```

profile of v0, /device:TPU:0, one launch (start us, length us, event | category | flops | bytes accessed | tf_op | source)
XLA Modules:
  0.0 121.1 jit_solution(8071006151488944462)
XLA Ops:
  0.0 0.9 reduce-window.8
  0.9 1.3 %fusion.23 = (s32[]{:T(128)}, s32[]{:T(128)}, s32[4]{0:T(128)S(1)}) fusion(s32[4]{0:T(128)} %param.9, s32[]{:T(128)S(6)} %axis_index.23, s32[4,1]{0,1:T(1,128)S(1)} %reduce-window.8), kind=kLoop, calls=%fused_computation.78 | loop fusion | flops 26 | bytes 60 | tf_op jit(solution)/shard_map/reduce_sum | solution.py:31
  2.3 0.6 gather_fusion
  3.0 0.7 copy.111
  3.7 15.1 %all_gather.9 = bf16[16,1,1664]{2,1,0:T(2,128)(2,1)S(1)} all-gather(bf16[4,1,1664]{2,1,0:T(2,128)(2,1)S(1)} %copy.111), channel_id=1, replica_groups=mesh['video'=2,'block'=4,'band'=2,'chan'=2] {'block'}, dimensions={0}, use_global_device_ids=true | all-gather | bytes 66560 | tf_op jit(solution)/shard_map/all_gather | solution.py:133
  18.9 0.6 gather_fusion.1
  19.5 1.3 %collective-permute-start.1 = (bf16[6,1,1664]{2,0,1:T(8,128)(2,1)S(1)}, bf16[6,1,1664]{2,0,1:T(8,128)(2,1)S(1)}, u32[]{:S(2)}, u32[]{:S(2)}) collective-permute-start(bf16[6,1,1664]{2,0,1:T(8,128)(2,1)S(1)} %fusion.21), channel_id=1, source_target_pairs={{2,0},{3,1},{6,4},{7,5},{10,8},{11,9},{14,12},{15,13},{18,16},{19,... | collective-permute-start | bytes 59912 | tf_op jit(solution)/shard_map/ppermute | solution.py:22
  20.8 4.5 %collective-permute-start = (bf16[6,1,1664]{2,0,1:T(8,128)(2,1)S(1)}, bf16[6,1,1664]{2,0,1:T(8,128)(2,1)S(1)}, u32[]{:S(2)}, u32[]{:S(2)}) collective-permute-start(bf16[6,1,1664]{2,0,1:T(8,128)(2,1)S(1)} %fusion.21), channel_id=1, source_target_pairs={{0,2},{1,3},{4,6},{5,7},{8,10},{9,11},{12,14},{13,15},{16,18},{17,... | collective-permute-start | bytes 59912 | tf_op jit(solution)/shard_map/ppermute | solution.py:20
  25.6 0.8 fusion.36
  26.4 3.6 %fusion.32 = (bf16[1,1,3,384,192]{3,4,2,1,0:T(8,128)(2,1)S(1)}, bf16[1,1,3,384,192]{3,4,2,1,0:T(8,128)(2,1)S(1)}, bf16[1,1,3,384,192]{3,4,2,1,0:T(8,128)(2,1)S(1...) fusion(bf16[3,3,3,384,192]{3,4,2,1,0:T(8,128)(2,1)} %param.13), kind=kLoop, calls=%fused_computation.95 | loop fusion | bytes 7962624 | tf_op jit(solution)/shard_map/slice | solution.py:109
  29.9 0.8 constant_dynamic-slice_fusion
  30.8 1.8 %compare_and_fusion.1 = (pred[4]{0:T(512)(128)(4,1)}, pred[4]{0:T(512)(128)(4,1)}) fusion(s32[]{:T(128)} %get-tuple-element.10, s32[]{:T(128)} %get-tuple-element.9), kind=kLoop, calls=%fused_computation.71 | loop fusion | flops 52 | bytes 16 | tf_op jit(solution)/shard_map/jit(_take)/and | solution.py:159
  32.6 0.6 add_compare_fusion
  33.2 0.7 dynamic_slice.11
  33.8 0.7 dynamic_slice.10
  35.1 1.3 %fusion.35 = (bf16[4,1,104,16]{3,2,0,1:T(8,128)(2,1)}, bf16[4,1,104,16]{3,2,0,1:T(8,128)(2,1)}, bf16[4,1,104,16]{3,2,0,1:T(8,128)(2,1)}, bf16[4,1,104,16]{3,2,0,...) fusion(bf16[6,3,106,16]{3,2,0,1:T(8,128)(2,1)S(1)} %fusion.14), kind=kLoop, calls=%fused_computation.98 | loop fusion | bytes 479232 | tf_op jit(solution)/shard_map/slice | solution.py:74
  36.5 0.6 fusion.37
  37.2 0.8 slice.234
  38.0 0.8 slice.238
  38.8 1.5 %slice.245 = bf16[4,1,104,16]{3,2,0,1:T(8,128)(2,1)} reshape(bf16[4,1,1664]{2,0,1:T(4,128)(2,1)} %get-tuple-element.73) | data formatting | bytes 26624 | tf_op jit(solution)/shard_map/slice | solution.py:74
  40.3 0.8 slice.249
  41.1 1.5 %slice.256 = bf16[4,1,104,16]{3,2,0,1:T(8,128)(2,1)} reshape(bf16[4,1,1664]{2,0,1:T(4,128)(2,1)} %get-tuple-element.72) | data formatting | bytes 26624 | tf_op jit(solution)/shard_map/slice | solution.py:74
  42.6 4.0 %concatenate.44 = bf16[4,1,104,432]{3,2,0,1:T(8,128)(2,1)} concatenate(bf16[4,1,104,16]{3,2,0,1:T(8,128)(2,1)} %get-tuple-element.68, bf16[4,1,104,16]{3,2,0,1:T(8,128)(2,1)S(1)} %slice.227, bf16[4,1,104,16]{3,2,0,1:T(8,128)(2,1)} %get-tuple-element.67, bf16[4,1,104,16]{3,2,0,1:T(8,128)(2,1)} %get-tuple-element.66, bf16[4,1,104,16]{3,2,0,1:T(8,128)(2,1)S(1)} %copy-done.18, ...), dimensions={3} | concatenate | bytes 718848 | tf_op jit(solution)/shard_map/concatenate | solution.py:81
  46.6 2.2 %fusion.30 = (f32[4,192]{1,0:T(4,128)S(1)}, f32[4,192]{1,0:T(4,128)S(1)}, f32[4,104,192]{1,2,0:T(8,128)}) fusion(bf16[432,192,1]{1,0,2:T(8,128)(2,1)} %bitcast.174, bf16[4,1,104,432]{3,2,0,1:T(8,128)(2,1)} %concatenate.44), kind=kOutput, calls=%fused_computation.93 | convolution fusion | flops 69407232 | bytes 850944 | tf_op jit(solution)/shard_map/dot_general | solution.py:82
  49.1 4.9 %all-reduce.3 = (f32[4,16]{1,0:T(4,128)S(1)}, f32[4,16]{1,0:T(4,128)S(1)}) all-reduce(f32[4,16]{1,0:T(4,128)S(1)} %reduce_sum.88, f32[4,16]{1,0:T(4,128)S(1)} %reduce_sum.85), channel_id=1, replica_groups=mesh['video'=2,'block'=4,'band'=2,'chan'=2] {'band'}, use_global_device_ids=true, to_apply=%region_9.10 | all-reduce | flops 128 | bytes 1024 | tf_op jit(solution)/shard_map/psum | solution.py:48
  54.4 1.3 %select_bitcast_fusion = bf16[4,1,104,192]{2,3,0,1:T(8,128)(2,1)S(1)} fusion(f32[192]{0:T(256)S(1)} %copy-done.19, f32[192]{0:T(256)S(1)} %copy-done.20, f32[4,192]{1,0:T(4,128)S(1)} %mul.122, f32[4,104,192]{1,2,0:T(8,128)} %get-tuple-element.83, f32[4,192]{1,0:T(4,128)S(1)} %sub.66, pred[4]{0:T(512)(128)(4,1)S(1)} %copy-done.27), kind=kLoop, calls=%fused_computation.52 | loop fusion | flops 798720 | bytes 486916 | tf_op jit(solution)/shard_map/jit(_where)/select_n | solution.py:148
  55.8 1.3 %collective-permute-start.3 = (bf16[4,1,104,192]{2,3,0,1:T(8,128)(2,1)S(1)}, bf16[4,1,104,192]{2,3,0,1:T(8,128)(2,1)S(1)}, u32[]{:S(2)}, u32[]{:S(2)}) collective-permute-start(bf16[4,1,104,192]{2,3,0,1:T(8,128)(2,1)S(1)} %select_bitcast_fusion), channel_id=1, source_target_pairs={{2,0},{3,1},{6,4},{7,5},{10,8},{11,9},{14,12},{15,13},{18,16},{19,... | collective-permute-start | bytes 479240 | tf_op jit(solution)/shard_map/ppermute | solution.py:22
  57.1 4.6 %collective-permute-start.2 = (bf16[4,1,104,192]{2,3,0,1:T(8,128)(2,1)S(1)}, bf16[4,1,104,192]{2,3,0,1:T(8,128)(2,1)S(1)}, u32[]{:S(2)}, u32[]{:S(2)}) collective-permute-start(bf16[4,1,104,192]{2,3,0,1:T(8,128)(2,1)S(1)} %select_bitcast_fusion), channel_id=1, source_target_pairs={{0,2},{1,3},{4,6},{5,7},{8,10},{9,11},{12,14},{13,15},{16,18},{17,... | collective-permute-start | bytes 479240 | tf_op jit(solution)/shard_map/ppermute | solution.py:20
  61.7 0.6 fusion.27
  62.3 0.4 copy.114
  62.7 0.8 copy.138
  63.8 0.4 copy.116
  64.2 0.8 copy.139
  65.3 0.4 copy.118
  65.7 0.8 copy.140
  66.6 0.4 copy.120
  67.0 0.8 copy.141
  67.8 0.4 copy.122
  68.2 0.8 copy.142
  69.0 0.4 copy.124
  69.4 0.8 copy.143
  70.2 0.4 copy.126
  70.6 0.8 copy.144
  71.4 0.4 copy.128
  71.8 0.8 copy.145
  73.0 0.8 copy.146
  74.2 2.8 %all_gather.10 = bf16[4,3,106,384]{2,3,0,1:T(8,128)(2,1)S(1)} all-gather(bf16[4,3,106,192]{2,3,0,1:T(8,128)(2,1)S(1)} %fusion.12), channel_id=1, replica_groups=mesh['video'=2,'block'=4,'band'=2,'chan'=2] {'chan'}, dimensions={3}, use_global_device_ids=true | all-gather | bytes 1465344 | tf_op jit(solution)/shard_map/all_gather | solution.py:117
  77.4 2.3 %fusion.33 = (bf16[2,1,104,384]{2,3,0,1:T(8,128)(2,1)S(1)}, bf16[2,1,104,384]{2,3,0,1:T(8,128)(2,1)}, bf16[2,1,104,384]{2,3,0,1:T(8,128)(2,1)}, bf16[2,1,104,384...) fusion(bf16[4,3,106,384]{2,3,0,1:T(8,128)(2,1)S(1)} %all_gather.10), kind=kLoop, calls=%fused_computation.96 | loop fusion | bytes 6070272 | tf_op jit(solution)/shard_map/slice | solution.py:98
  79.8 1.0 copy.113
  81.2 0.6 copy-done.15
  82.3 1.1 pad_maximum_fusion.3
  83.7 1.0 pad_maximum_fusion.4
  85.1 1.2 %pad_maximum_fusion.5 = bf16[2,1,104,1152]{2,3,0,1:T(8,128)(2,1)S(1)} fusion(bf16[2,1,104,384]{2,3,0,1:T(8,128)(2,1)} %get-tuple-element.33, bf16[2,1,104,384]{2,3,0,1:T(8,128)(2,1)} %get-tuple-element.34, bf16[2,1,104,384]{2,3,0,1:T(8,128)(2,1)} %get-tuple-element.35), kind=kLoop, calls=%fused_computation.34 | loop fusion | flops 1437696 | bytes 958464 | tf_op jit(solution)/shard_map/concatenate | solution.py:106
  86.6 1.2 %pad_maximum_fusion.6 = bf16[2,1,104,1152]{2,3,0,1:T(8,128)(2,1)S(1)} fusion(bf16[2,1,104,384]{2,3,0,1:T(8,128)(2,1)} %get-tuple-element.30, bf16[2,1,104,384]{2,3,0,1:T(8,128)(2,1)} %get-tuple-element.31, bf16[2,1,104,384]{2,3,0,1:T(8,128)(2,1)} %get-tuple-element.32), kind=kLoop, calls=%fused_computation.35 | loop fusion | flops 1437696 | bytes 958464 | tf_op jit(solution)/shard_map/concatenate | solution.py:106
  87.8 1.1 copy.125
  88.9 1.2 %pad_maximum_fusion.7 = bf16[2,1,104,1152]{2,3,0,1:T(8,128)(2,1)S(1)} fusion(bf16[2,1,104,384]{2,3,0,1:T(8,128)(2,1)} %get-tuple-element.27, bf16[2,1,104,384]{2,3,0,1:T(8,128)(2,1)} %get-tuple-element.28, bf16[2,1,104,384]{2,3,0,1:T(8,128)(2,1)} %get-tuple-element.29), kind=kLoop, calls=%fused_computation.36 | loop fusion | flops 1437696 | bytes 958464 | tf_op jit(solution)/shard_map/concatenate | solution.py:106
  90.2 1.0 copy.127
  91.2 1.1 pad_maximum_fusion.8
  92.3 1.0 copy.129
  93.4 1.6 %fusion.39 = f32[208,192]{0,1:T(8,128)S(1)} fusion(bf16[208,1152]{1,0:T(8,128)(2,1)} %bitcast.162, bf16[1152,192]{0,1:T(8,128)(2,1)} %bitcast.163), kind=kOutput, calls=%fused_computation.102 | convolution fusion | flops 92012544 | bytes 1081344 | tf_op jit(solution)/shard_map/dot_general | solution.py:107
  99.9 4.9 %all-reduce.2 = (f32[2,16]{1,0:T(2,128)S(1)}, f32[2,16]{1,0:T(2,128)S(1)}) all-reduce(f32[2,16]{1,0:T(2,128)S(1)} %copy.133, f32[2,16]{1,0:T(2,128)S(1)} %copy.131), channel_id=1, replica_groups=mesh['video'=2,'block'=4,'band'=2,'chan'=2] {'band'}, use_global_device_ids=true, to_apply=%region_13.14 | all-reduce | flops 64 | bytes 512 | tf_op jit(solution)/shard_map/psum | solution.py:48
  105.4 14.3 %all_gather.11 = bf16[8,1,104,192]{2,3,1,0:T(8,128)(2,1)S(1)} all-gather(bf16[2,1,104,192]{2,3,1,0:T(8,128)(2,1)S(1)} %multiply_convert_fusion.1), channel_id=1, replica_groups=mesh['video'=2,'block'=4,'band'=2,'chan'=2] {'block'}, dimensions={0}, use_global_device_ids=true | all-gather | bytes 399360 | tf_op jit(solution)/shard_map/all_gather | solution.py:157
  119.8 0.6 gather_fusion.2
  120.4 0.8 fusion.17
  (115 shorter events, 10.7 us)
Async XLA Ops:
  0.0 29.9 %copy-start = (bf16[3,3,3,16,384]{4,3,2,1,0:T(8,128)(2,1)S(1)}, bf16[3,3,3,16,384]{4,3,2,1,0:T(8,128)(2,1)}, u32[]{:S(2)}) copy-start(bf16[3,3,3,16,384]{4,3,2,1,0:T(8,128)(2,1)} %param.10) | copy-start | bytes 995332
  19.5 15.0 %collective-permute-start.1 = (bf16[6,1,1664]{2,0,1:T(8,128)(2,1)S(1)}, bf16[6,1,1664]{2,0,1:T(8,128)(2,1)S(1)}, u32[]{:S(2)}, u32[]{:S(2)}) collective-permute-start(bf16[6,1,1664]{2,0,1:T(8,128)(2,1)S(1)} %fusion.21), channel_id=1, source_target_pairs={{2,0},{3,1},{6,4},{7,5},{10,8},{11,9},{14,12},{15,13},{18,16},{19,... | collective-permute-start | bytes 59912 | tf_op jit(solution)/shard_map/ppermute | solution.py:22
  20.8 13.9 %collective-permute-start = (bf16[6,1,1664]{2,0,1:T(8,128)(2,1)S(1)}, bf16[6,1,1664]{2,0,1:T(8,128)(2,1)S(1)}, u32[]{:S(2)}, u32[]{:S(2)}) collective-permute-start(bf16[6,1,1664]{2,0,1:T(8,128)(2,1)S(1)} %fusion.21), channel_id=1, source_target_pairs={{0,2},{1,3},{4,6},{5,7},{8,10},{9,11},{12,14},{13,15},{16,18},{17,... | collective-permute-start | bytes 59912 | tf_op jit(solution)/shard_map/ppermute | solution.py:20
  26.4 6.8 %copy-start.25 = (f32[384]{0:T(512)S(1)}, f32[384]{0:T(512)}, u32[]{:S(2)}) copy-start(f32[384]{0:T(512)} %param.12) | copy-start | bytes 4612
  26.4 7.5 %copy-start.26 = (f32[384]{0:T(512)S(1)}, f32[384]{0:T(512)}, u32[]{:S(2)}) copy-start(f32[384]{0:T(512)} %param.11) | copy-start | bytes 4612
  35.1 7.5 %copy-start.16 = (bf16[4,1,104,16]{3,2,0,1:T(8,128)(2,1)S(1)}, bf16[4,1,104,16]{3,2,0,1:T(8,128)(2,1)}, u32[]{:S(2)}) copy-start(bf16[4,1,104,16]{3,2,0,1:T(8,128)(2,1)} %get-tuple-element.69) | copy-start | bytes 39940
  35.1 7.5 %copy-start.17 = (bf16[4,1,104,16]{3,2,0,1:T(8,128)(2,1)S(1)}, bf16[4,1,104,16]{3,2,0,1:T(8,128)(2,1)}, u32[]{:S(2)}) copy-start(bf16[4,1,104,16]{3,2,0,1:T(8,128)(2,1)} %get-tuple-element.70) | copy-start | bytes 39940
  35.1 7.5 %copy-start.18 = (bf16[4,1,104,16]{3,2,0,1:T(8,128)(2,1)S(1)}, bf16[4,1,104,16]{3,2,0,1:T(8,128)(2,1)}, u32[]{:S(2)}) copy-start(bf16[4,1,104,16]{3,2,0,1:T(8,128)(2,1)} %get-tuple-element.71) | copy-start | bytes 39940
  46.5 7.9 %copy-start.19 = (f32[192]{0:T(256)S(1)}, f32[192]{0:T(256)}, u32[]{:S(2)}) copy-start(f32[192]{0:T(256)} %dynamic_slice.11) | copy-start | bytes 2308
  46.5 7.9 %copy-start.20 = (f32[192]{0:T(256)S(1)}, f32[192]{0:T(256)}, u32[]{:S(2)}) copy-start(f32[192]{0:T(256)} %dynamic_slice.10) | copy-start | bytes 2308
  46.5 7.9 %copy-start.27 = (pred[4]{0:T(512)(128)(4,1)S(1)}, pred[4]{0:T(512)(128)(4,1)}, u32[]{:S(2)}) copy-start(pred[4]{0:T(512)(128)(4,1)} %add_compare_fusion) | copy-start | bytes 16
  46.5 15.8 %copy-start.14 = (bf16[1,1,3,384,192]{3,4,2,1,0:T(8,128)(2,1)S(1)}, bf16[1,1,3,384,192]{3,4,2,1,0:T(8,128)(2,1)}, u32[]{:S(2)}) copy-start(bf16[1,1,3,384,192]{3,4,2,1,0:T(8,128)(2,1)} %get-tuple-element.22) | copy-start | bytes 1327108
  55.8 18.1 %collective-permute-start.3 = (bf16[4,1,104,192]{2,3,0,1:T(8,128)(2,1)S(1)}, bf16[4,1,104,192]{2,3,0,1:T(8,128)(2,1)S(1)}, u32[]{:S(2)}, u32[]{:S(2)}) collective-permute-start(bf16[4,1,104,192]{2,3,0,1:T(8,128)(2,1)S(1)} %select_bitcast_fusion), channel_id=1, source_target_pairs={{2,0},{3,1},{6,4},{7,5},{10,8},{11,9},{14,12},{15,13},{18,16},{19,... | collective-permute-start | bytes 479240 | tf_op jit(solution)/shard_map/ppermute | solution.py:22
  57.1 16.8 %collective-permute-start.2 = (bf16[4,1,104,192]{2,3,0,1:T(8,128)(2,1)S(1)}, bf16[4,1,104,192]{2,3,0,1:T(8,128)(2,1)S(1)}, u32[]{:S(2)}, u32[]{:S(2)}) collective-permute-start(bf16[4,1,104,192]{2,3,0,1:T(8,128)(2,1)S(1)} %select_bitcast_fusion), channel_id=1, source_target_pairs={{0,2},{1,3},{4,6},{5,7},{8,10},{9,11},{12,14},{13,15},{16,18},{17,... | collective-permute-start | bytes 479240 | tf_op jit(solution)/shard_map/ppermute | solution.py:20
  62.7 1.1 copy-start.13
  64.2 1.1 copy-start.12
  80.9 0.9 copy-start.15
  93.4 1.6 %copy-start.4 = (bf16[24,8,3,384]{3,1,2,0:T(8,128)(2,1)S(1)}, bf16[24,8,3,384]{3,1,2,0:T(8,128)(2,1)}, u32[]{:S(2)}) copy-start(bf16[24,8,3,384]{3,1,2,0:T(8,128)(2,1)} %copy.139) | copy-start | bytes 1327108
  93.4 1.9 %copy-start.5 = (bf16[24,8,3,384]{3,1,2,0:T(8,128)(2,1)S(1)}, bf16[24,8,3,384]{3,1,2,0:T(8,128)(2,1)}, u32[]{:S(2)}) copy-start(bf16[24,8,3,384]{3,1,2,0:T(8,128)(2,1)} %copy.140) | copy-start | bytes 1327108
  94.9 1.0 copy-start.6
  95.3 1.0 copy-start.7
  96.0 1.0 copy-start.8
  96.3 1.1 copy-start.1
  96.4 1.2 copy-start.9
  97.0 1.1 copy-start.2
  97.0 1.2 %copy-start.10 = (bf16[24,8,3,384]{3,1,2,0:T(8,128)(2,1)S(1)}, bf16[24,8,3,384]{3,1,2,0:T(8,128)(2,1)}, u32[]{:S(2)}) copy-start(bf16[24,8,3,384]{3,1,2,0:T(8,128)(2,1)} %copy.145) | copy-start | bytes 1327108
  97.5 1.1 copy-start.3
  97.5 1.2 %copy-start.11 = (bf16[24,8,3,384]{3,1,2,0:T(8,128)(2,1)S(1)}, bf16[24,8,3,384]{3,1,2,0:T(8,128)(2,1)}, u32[]{:S(2)}) copy-start(bf16[24,8,3,384]{3,1,2,0:T(8,128)(2,1)} %copy.146) | copy-start | bytes 1327108
  98.8 6.4 %copy-start.23 = (f32[192]{0:T(256)S(1)}, f32[192]{0:T(256)}, u32[]{:S(2)}) copy-start(f32[192]{0:T(256)} %param.15) | copy-start | bytes 2308
  98.8 6.4 %copy-start.24 = (f32[192]{0:T(256)S(1)}, f32[192]{0:T(256)}, u32[]{:S(2)}) copy-start(f32[192]{0:T(256)} %param.14) | copy-start | bytes 2308
  99.1 21.3 %copy-start.21 = (pred[4]{0:T(512)(128)(4,1)S(1)}, pred[4]{0:T(512)(128)(4,1)}, u32[]{:S(2)}) copy-start(pred[4]{0:T(512)(128)(4,1)} %get-tuple-element.84) | copy-start | bytes 16
  99.1 21.3 %copy-start.22 = (pred[4]{0:T(512)(128)(4,1)S(1)}, pred[4]{0:T(512)(128)(4,1)}, u32[]{:S(2)}) copy-start(pred[4]{0:T(512)(128)(4,1)} %get-tuple-element.85) | copy-start | bytes 16
where the time goes:
time: 122 us; the launch traced here: 121 us
  local copies, waits for them, and re-layouts  44.2 us (36%)
  blocking collectives  42.1 us (35%)
  other arithmetic  16.3 us (13%)
  starting transfers between devices  11.7 us (10%)
  matrix products  6.32 us (5%)
    all_gather x1, blocking collectives, shards(): all_slots = lax.all_gather(latents, 'block', axis=0, tiled=True)  15.1 us
    all_gather x1, blocking collectives, shards(): piece = lax.all_gather(even_norm, 'block', axis=0, tiled=True)  14.3 us
    unnamed x67, local copies, waits for them, and re-layouts  11 us
    psum x2, blocking collectives, group_silu(): lax.psum((jnp.sum(grouped, axis=(1, 3)), jnp.sum(grouped * grouped, axis=...  9.83 us
    ppermute x2, starting transfers between devices, with_halo(): lax.ppermute(tail, axis, [(i, (i + 1) % count) for i in range(ends)])  9.11 us
    slice x10, local copies, waits for them, and re-layouts, latent_conv(): latent_grid[step_t:step_t + out_frames, step_y:step_y + band_rows, step_x...  8.19 us
    concatenate x9, other arithmetic, weighted_taps(): stacked = jnp.concatenate(patches, axis=-1).reshape(-1, 3 * in_width)  7.39 us
    slice x10, local copies, waits for them, and re-layouts, weighted_taps(): kernel[step_t, step_y].reshape(3 * in_width, out_width)  6.99 us
  transfers between devices with their start and end apart: 4, of which 0 were waited for; matrix products, arithmetic and copies ran while one was open for 17% of the time, Pallas kernels for 0%

commit v1 on v0

--- a/solution.py
+++ b/solution.py
@@ -154,7 +154,16 @@
     slot_frames = my_start + slot_places
     slot_alive = slot_places < live_count
     initial = jnp.zeros((frames, band_rows, columns, half_width), jnp.bfloat16)
-    piece = lax.all_gather(even_norm, "block", axis=0, tiled=True)
+    ways = lax.axis_size("block")
+    up = [(d, (d + 1) % ways) for d in range(ways)]
+    down = [(d, (d - 1) % ways) for d in range(ways)]
+    earlier, later = ([even_norm], [even_norm])
+    for _ in range(ways // 2):
+        earlier.append(lax.ppermute(earlier[-1], "block", up))
+    for _ in range((ways - 1) // 2):
+        later.append(lax.ppermute(later[-1], "block", down))
+    line = jnp.concatenate([*earlier[::-1], *later[1:]], axis=0)
+    piece = jnp.roll(line, (lax.axis_index("block") - ways // 2) * even_norm.shape[0], axis=0)
     valid = (slot_frames >= 0) & (slot_frames < piece.shape[0]) & slot_alive
     took = jnp.take(piece, jnp.clip(slot_frames, 0, piece.shape[0] - 1), axis=0)
     return jnp.where(valid[:, None, None, None], took, initial)

time: 122 us -> 113 us (0.926)
  blocking collectives: 42.1 us -> 28 us
  waiting for transfers between devices: 0.01 us -> 8.8 us
  local copies, waits for them, and re-layouts: 44.2 us -> 36.2 us
  starting transfers between devices: 11.7 us -> 17.1 us
  matrix products: 6.32 us -> 4.74 us
    all_gather x1 -> x0, blocking collectives: 14.3 us -> none  [shards(): piece = lax.all_gather(even_norm, 'block', axis=0, tiled=True)]
    ppermute x0 -> x3, waiting for transfers between devices: none -> 8.12 us  [the longest x2 8.12 us: shards(): earlier.append(lax.ppermute(earlier[-1], 'block', up))]
    slice x10, local copies, waits for them, and re-layouts: 8.19 us -> 1.87 us  [latent_conv(): latent_grid[step_t:step_t + out_frames, step_y:step_y + band_rows, step_x...]
    ppermute x0 -> x3, starting transfers between devices: none -> 4.13 us  [the longest x1 2.17 us: shards(): later.append(lax.ppermute(later[-1], 'block', down))]
    dot_general x1, matrix products: 2.2 us -> 0.63 us  [latent_conv(): jnp.dot(stacked, kernel.reshape(27 * lat_width, out_width), preferred_ele...]
    concatenate x1, local copies, waits for them, and re-layouts: 3.95 us -> 2.54 us  [latent_conv(): stacked = jnp.concatenate(patches, axis=-1).reshape(-1, 27 * lat_width)]
    concatenate x0 -> x1, local copies, waits for them, and re-layouts: none -> 1.4 us  [shards(): jnp.roll(line, (lax.axis_index('block') - ways // 2) * even_norm.shape[0]...]
    ppermute x2, starting transfers between devices: 9.11 us -> 10.4 us  [with_halo(): lax.ppermute(tail, axis, [(i, (i + 1) % count) for i in range(ends)])]
  transfers between devices with their start and end apart: 4 -> 7, of which waited for: 0 -> 3; matrix products, arithmetic and copies ran while one was open for 17% -> 16% of each run, Pallas kernels for 0% -> 0%
where the time goes in v1:
time: 113 us; the launch traced here: 112 us
  local copies, waits for them, and re-layouts  36.2 us (32%)
  blocking collectives  28 us (25%)
  starting transfers between devices  17.1 us (15%)
  other arithmetic  16.4 us (15%)
  waiting for transfers between devices  8.8 us (8%)
  matrix products  4.74 us (4%)
    all_gather x1, blocking collectives, shards(): all_slots = lax.all_gather(latents, 'block', axis=0, tiled=True)  15.1 us
    ppermute x2, starting transfers between devices, with_halo(): lax.ppermute(tail, axis, [(i, (i + 1) % count) for i in range(ends)])  10.4 us
    psum x2, blocking collectives, group_silu(): lax.psum((jnp.sum(grouped, axis=(1, 3)), jnp.sum(grouped * grouped, axis=...  10.1 us
    unnamed x45, local copies, waits for them, and re-layouts  9.98 us
    ppermute x2, waiting for transfers between devices, shards(): earlier.append(lax.ppermute(earlier[-1], 'block', up))  8.12 us
    slice x10, local copies, waits for them, and re-layouts, weighted_taps(): kernel[step_t, step_y].reshape(3 * in_width, out_width)  7.9 us
    concatenate x9, other arithmetic, weighted_taps(): stacked = jnp.concatenate(patches, axis=-1).reshape(-1, 3 * in_width)  7.29 us
    concatenate x9, local copies, waits for them, and re-layouts, weighted_taps(): stacked = jnp.concatenate(patches, axis=-1).reshape(-1, 3 * in_width)  5.64 us
  transfers between devices with their start and end apart: 7, of which 3 were waited for; matrix products, arithmetic and copies ran while one was open for 16% of the time, Pallas kernels for 0%

profile of v1, /device:TPU:0, one launch (start us, length us, event | category | flops | bytes accessed | tf_op | source)
XLA Modules:
  0.0 112.0 jit_solution(9276626293088189438)
XLA Ops:
  0.0 0.9 reduce-window.8
  0.9 1.3 %fusion.21 = (s32[]{:T(128)}, s32[]{:T(128)}, s32[4]{0:T(128)S(1)}) fusion(s32[4]{0:T(128)} %param.9, s32[]{:T(128)S(6)} %axis_index.27, s32[4,1]{0,1:T(1,128)S(1)} %reduce-window.8), kind=kLoop, calls=%fused_computation.76 | loop fusion | flops 26 | bytes 60 | tf_op jit(solution)/shard_map/reduce_sum | solution.py:31
  2.3 0.6 gather_fusion
  3.0 0.7 copy.119
  3.7 15.1 %all_gather.6 = bf16[16,1,1664]{2,1,0:T(2,128)(2,1)S(1)} all-gather(bf16[4,1,1664]{2,1,0:T(2,128)(2,1)S(1)} %copy.119), channel_id=1, replica_groups=mesh['video'=2,'block'=4,'band'=2,'chan'=2] {'block'}, dimensions={0}, use_global_device_ids=true | all-gather | bytes 66560 | tf_op jit(solution)/shard_map/all_gather | solution.py:133
  18.8 0.6 gather_fusion.1
  19.5 1.3 %collective-permute-start.1 = (bf16[6,1,1664]{2,0,1:T(8,128)(2,1)S(1)}, bf16[6,1,1664]{2,0,1:T(8,128)(2,1)S(1)}, u32[]{:S(2)}, u32[]{:S(2)}) collective-permute-start(bf16[6,1,1664]{2,0,1:T(8,128)(2,1)S(1)} %fusion.19), channel_id=1, source_target_pairs={{2,0},{3,1},{6,4},{7,5},{10,8},{11,9},{14,12},{15,13},{18,16},{19,... | collective-permute-start | bytes 59912 | tf_op jit(solution)/shard_map/ppermute | solution.py:22
  20.8 4.5 %collective-permute-start = (bf16[6,1,1664]{2,0,1:T(8,128)(2,1)S(1)}, bf16[6,1,1664]{2,0,1:T(8,128)(2,1)S(1)}, u32[]{:S(2)}, u32[]{:S(2)}) collective-permute-start(bf16[6,1,1664]{2,0,1:T(8,128)(2,1)S(1)} %fusion.19), channel_id=1, source_target_pairs={{0,2},{1,3},{4,6},{5,7},{8,10},{9,11},{12,14},{13,15},{16,18},{17,... | collective-permute-start | bytes 59912 | tf_op jit(solution)/shard_map/ppermute | solution.py:20
  26.2 0.7 collective-permute-done
  27.2 1.0 fusion.33
  29.1 2.5 %concatenate.50 = bf16[4,1,104,432]{3,2,0,1:T(8,128)(2,1)S(1)} concatenate(bf16[4,1,104,16]{3,2,0,1:T(8,128)(2,1)} %get-tuple-element.68, bf16[4,1,104,16]{3,2,0,1:T(8,128)(2,1)S(1)} %slice.227, bf16[4,1,104,16]{3,2,0,1:T(8,128)(2,1)} %get-tuple-element.67, bf16[4,1,104,16]{3,2,0,1:T(8,128)(2,1)} %get-tuple-element.66, bf16[4,1,104,16]{3,2,0,1:T(8,128)(2,1)S(1)} %get-tuple-element.71, ...), dimensions={3} | concatenate | bytes 718848 | tf_op jit(solution)/shard_map/concatenate | solution.py:81
  31.7 0.6 fusion.28
  32.7 5.2 %all-reduce.3 = (f32[4,16]{1,0:T(4,128)S(1)}, f32[4,16]{1,0:T(4,128)S(1)}) all-reduce(f32[4,16]{1,0:T(4,128)S(1)} %reduce_sum.88, f32[4,16]{1,0:T(4,128)S(1)} %reduce_sum.85), channel_id=1, replica_groups=mesh['video'=2,'block'=4,'band'=2,'chan'=2] {'band'}, use_global_device_ids=true, to_apply=%region_9.10 | all-reduce | flops 128 | bytes 1024 | tf_op jit(solution)/shard_map/psum | solution.py:48
  38.2 1.0 select_bitcast_fusion
  39.3 1.3 %collective-permute-start.3 = (bf16[4,1,104,192]{2,3,0,1:T(8,128)(2,1)}, bf16[4,1,104,192]{2,3,0,1:T(8,128)(2,1)}, u32[]{:S(2)}, u32[]{:S(2)}) collective-permute-start(bf16[4,1,104,192]{2,3,0,1:T(8,128)(2,1)} %select_bitcast_fusion), channel_id=1, source_target_pairs={{2,0},{3,1},{6,4},{7,5},{10,8},{11,9},{14,12},{15,13},{18,16},{19,... | collective-permute-start | bytes 479240 | tf_op jit(solution)/shard_map/ppermute | solution.py:22
  40.6 5.9 %collective-permute-start.2 = (bf16[4,1,104,192]{2,3,0,1:T(8,128)(2,1)}, bf16[4,1,104,192]{2,3,0,1:T(8,128)(2,1)}, u32[]{:S(2)}, u32[]{:S(2)}) collective-permute-start(bf16[4,1,104,192]{2,3,0,1:T(8,128)(2,1)} %select_bitcast_fusion), channel_id=1, source_target_pairs={{0,2},{1,3},{4,6},{5,7},{8,10},{9,11},{12,14},{13,15},{16,18},{17,... | collective-permute-start | bytes 479240 | tf_op jit(solution)/shard_map/ppermute | solution.py:20
  46.4 3.4 %fusion.30 = (bf16[1,1,3,384,192]{3,4,2,1,0:T(8,128)(2,1)S(1)}, bf16[1,1,3,384,192]{3,4,2,1,0:T(8,128)(2,1)S(1)}, bf16[1,1,3,384,192]{3,4,2,1,0:T(8,128)(2,1)S(1...) fusion(bf16[3,3,3,384,192]{3,4,2,1,0:T(8,128)(2,1)} %param.13), kind=kLoop, calls=%fused_computation.94 | loop fusion | bytes 7962624 | tf_op jit(solution)/shard_map/slice | solution.py:109
  49.9 1.4 %copy.122 = bf16[1,1,3,384,192]{3,2,4,1,0:T(4,128)(2,1)S(1)} copy(bf16[1,1,3,384,192]{3,4,2,1,0:T(8,128)(2,1)} %get-tuple-element.22) | data formatting | bytes 884736 | tf_op jit(solution)/shard_map/slice | solution.py:109
  51.3 0.8 copy.148
  52.4 0.4 copy.124
  52.8 0.8 copy.149
  53.6 0.4 copy.126
  54.0 0.8 copy.150
  54.9 0.4 copy.128
  55.2 0.8 copy.151
  56.1 0.4 copy.130
  56.5 0.8 copy.152
  57.3 0.4 copy.132
  57.7 0.8 copy.153
  58.5 0.4 copy.134
  58.9 0.8 copy.154
  59.7 0.4 copy.136
  60.1 0.8 copy.155
  60.9 0.4 copy.138
  61.3 0.8 copy.156
  62.1 0.6 fusion.25
  62.7 1.4 %fusion.12 = bf16[4,3,106,192]{2,3,0,1:T(8,128)(2,1)S(1)} fusion(bf16[4,1,104,192]{2,3,0,1:T(8,128)(2,1)} %collective-permute-done.3, bf16[4,1,104,192]{2,3,0,1:T(8,128)(2,1)} %select_bitcast_fusion, bf16[4,1,104,192]{2,3,0,1:T(8,128)(2,1)} %collective-permute-done.2), kind=kLoop, calls=%fused_computation.28 | loop fusion | flops 2930688 | bytes 967680 | tf_op jit(solution)/shard_map/concatenate | solution.py:18
  64.1 2.8 %all_gather.7 = bf16[4,3,106,384]{2,3,0,1:T(8,128)(2,1)S(1)} all-gather(bf16[4,3,106,192]{2,3,0,1:T(8,128)(2,1)S(1)} %fusion.12), channel_id=1, replica_groups=mesh['video'=2,'block'=4,'band'=2,'chan'=2] {'chan'}, dimensions={3}, use_global_device_ids=true | all-gather | bytes 1465344 | tf_op jit(solution)/shard_map/all_gather | solution.py:117
  67.0 0.3 fusion.32
  67.3 2.2 %fusion.31 = (bf16[2,1,104,384]{2,3,0,1:T(8,128)(2,1)S(1)}, bf16[2,1,104,384]{2,3,0,1:T(8,128)(2,1)}, bf16[2,1,104,384]{2,3,0,1:T(8,128)(2,1)}, bf16[2,1,104,384...) fusion(bf16[4,3,106,384]{2,3,0,1:T(8,128)(2,1)S(1)} %all_gather.7), kind=kLoop, calls=%fused_computation.95 | loop fusion | bytes 6070272 | tf_op jit(solution)/shard_map/slice | solution.py:98
  69.6 1.0 copy.121
  71.5 1.0 pad_maximum_fusion.3
  72.8 1.0 pad_maximum_fusion.4
  74.1 1.2 %pad_maximum_fusion.5 = bf16[2,1,104,1152]{2,3,0,1:T(8,128)(2,1)S(1)} fusion(bf16[2,1,104,384]{2,3,0,1:T(8,128)(2,1)} %get-tuple-element.33, bf16[2,1,104,384]{2,3,0,1:T(8,128)(2,1)} %get-tuple-element.34, bf16[2,1,104,384]{2,3,0,1:T(8,128)(2,1)} %get-tuple-element.35), kind=kLoop, calls=%fused_computation.34 | loop fusion | flops 1437696 | bytes 958464 | tf_op jit(solution)/shard_map/concatenate | solution.py:106
  75.7 1.2 %pad_maximum_fusion.6 = bf16[2,1,104,1152]{2,3,0,1:T(8,128)(2,1)S(1)} fusion(bf16[2,1,104,384]{2,3,0,1:T(8,128)(2,1)} %get-tuple-element.30, bf16[2,1,104,384]{2,3,0,1:T(8,128)(2,1)} %get-tuple-element.31, bf16[2,1,104,384]{2,3,0,1:T(8,128)(2,1)} %get-tuple-element.32), kind=kLoop, calls=%fused_computation.35 | loop fusion | flops 1437696 | bytes 958464 | tf_op jit(solution)/shard_map/concatenate | solution.py:106
  76.9 1.1 copy.133
  78.0 1.2 %pad_maximum_fusion.7 = bf16[2,1,104,1152]{2,3,0,1:T(8,128)(2,1)S(1)} fusion(bf16[2,1,104,384]{2,3,0,1:T(8,128)(2,1)} %get-tuple-element.27, bf16[2,1,104,384]{2,3,0,1:T(8,128)(2,1)} %get-tuple-element.28, bf16[2,1,104,384]{2,3,0,1:T(8,128)(2,1)} %get-tuple-element.29), kind=kLoop, calls=%fused_computation.36 | loop fusion | flops 1437696 | bytes 958464 | tf_op jit(solution)/shard_map/concatenate | solution.py:106
  79.2 1.1 copy.135
  80.3 1.1 %pad_maximum_fusion.8 = bf16[2,1,104,1152]{2,3,0,1:T(8,128)(2,1)S(1)} fusion(bf16[2,1,104,384]{2,3,0,1:T(8,128)(2,1)} %get-tuple-element.25, bf16[2,1,104,384]{2,3,0,1:T(8,128)(2,1)} %get-tuple-element.26, bf16[2,1,104,384]{2,3,0,1:T(8,128)(2,1)S(1)} %get-tuple-element.24), kind=kLoop, calls=%fused_computation.37 | loop fusion | flops 1437696 | bytes 958464 | tf_op jit(solution)/shard_map/concatenate | solution.py:106
  81.4 1.0 copy.137
  82.5 1.6 %fusion.37 = f32[208,192]{0,1:T(8,128)S(1)} fusion(bf16[208,1152]{1,0:T(8,128)(2,1)} %bitcast.164, bf16[1152,192]{0,1:T(8,128)(2,1)} %bitcast.165), kind=kOutput, calls=%fused_computation.101 | convolution fusion | flops 92012544 | bytes 1081344 | tf_op jit(solution)/shard_map/dot_general | solution.py:107
  84.0 0.3 convolution_add_fusion.7
  84.7 0.3 copy-done.6
  85.8 0.3 copy-done.8
  89.0 4.9 %all-reduce.2 = (f32[2,16]{1,0:T(2,128)S(1)}, f32[2,16]{1,0:T(2,128)S(1)}) all-reduce(f32[2,16]{1,0:T(2,128)S(1)} %copy.141, f32[2,16]{1,0:T(2,128)S(1)} %copy.139), channel_id=1, replica_groups=mesh['video'=2,'block'=4,'band'=2,'chan'=2] {'band'}, use_global_device_ids=true, to_apply=%region_13.14 | all-reduce | flops 64 | bytes 512 | tf_op jit(solution)/shard_map/psum | solution.py:48
  94.5 1.0 fusion.18
  95.5 1.7 %collective-permute-start.4 = (bf16[2,1,104,192]{2,0,3,1:T(2,128)(2,1)S(1)}, bf16[2,1,104,192]{2,0,3,1:T(2,128)(2,1)S(1)}, u32[]{:S(2)}, u32[]{:S(2)}) collective-permute-start(bf16[2,1,104,192]{2,0,3,1:T(2,128)(2,1)S(1)} %fusion.18), channel_id=1, source_target_pairs={{0,4},{4,8},{8,12},{12,0},{1,5},{5,9},{9,13},{13,1},{2,6},{6,10},{... | collective-permute-start | bytes 239624 | tf_op jit(solution)/shard_map/ppermute | solution.py:162
  97.3 2.2 %collective-permute-start.6 = (bf16[2,1,104,192]{2,0,3,1:T(2,128)(2,1)S(1)}, bf16[2,1,104,192]{2,0,3,1:T(2,128)(2,1)S(1)}, u32[]{:S(2)}, u32[]{:S(2)}) collective-permute-start(bf16[2,1,104,192]{2,0,3,1:T(2,128)(2,1)S(1)} %fusion.18), channel_id=1, source_target_pairs={{0,12},{4,0},{8,4},{12,8},{1,13},{5,1},{9,5},{13,9},{2,14},{6,2},{... | collective-permute-start | bytes 239624 | tf_op jit(solution)/shard_map/ppermute | solution.py:164
  99.4 3.2 %collective-permute-done.4 = bf16[2,1,104,192]{2,0,3,1:T(2,128)(2,1)S(1)} collective-permute-done((bf16[2,1,104,192]{2,0,3,1:T(2,128)(2,1)S(1)}, bf16[2,1,104,192]{2,0,3,1:T(2,128)(2,1)S(1)}, u32[]{:S(2)}, u32[]{:S(2)}) %collective-permute-start.4) | collective-permute-done | bytes 79904 | tf_op jit(solution)/shard_map/ppermute | solution.py:162
  102.9 1.2 %compare_and_fusion.1 = (pred[4]{0:T(512)(128)(4,1)S(1)}, pred[4]{0:T(512)(128)(4,1)S(1)}) fusion(s32[]{:T(128)} %get-tuple-element.10, s32[]{:T(128)} %get-tuple-element.9), kind=kLoop, calls=%fused_computation.69 | loop fusion | flops 52 | bytes 16 | tf_op jit(solution)/shard_map/jit(_take)/and | solution.py:168
  104.1 5.0 %collective-permute-done.5 = bf16[2,1,104,192]{2,0,3,1:T(2,128)(2,1)S(1)} collective-permute-done((bf16[2,1,104,192]{2,0,3,1:T(2,128)(2,1)S(1)}, bf16[2,1,104,192]{2,0,3,1:T(2,128)(2,1)S(1)}, u32[]{:S(2)}, u32[]{:S(2)}) %collective-permute-start.5) | collective-permute-done | bytes 79904 | tf_op jit(solution)/shard_map/ppermute | solution.py:162
  109.0 1.4 %concatenate.61 = bf16[16,1,104,192]{2,0,3,1:T(8,128)(2,1)S(1)} concatenate(bf16[2,1,104,192]{2,0,3,1:T(2,128)(2,1)S(1)} %collective-permute-done.5, bf16[2,1,104,192]{2,0,3,1:T(2,128)(2,1)S(1)} %collective-permute-done.4, bf16[2,1,104,192]{2,0,3,1:T(2,128)(2,1)S(1)} %fusion.18, bf16[2,1,104,192]{2,0,3,1:T(2,128)(2,1)S(1)} %collective-permute-done.6, ...), dimensions={0} | concatenate | bytes 1277952 | tf_op jit(solution)/shard_map/jit(_roll_dynamic)/concatenate | solution.py:166
  110.6 0.6 gather_fusion.2
  111.2 0.8 fusion.17
  (103 shorter events, 9.9 us)
Async XLA Ops:
  0.0 25.7 %copy-start = (bf16[3,3,3,16,384]{4,3,2,1,0:T(8,128)(2,1)S(1)}, bf16[3,3,3,16,384]{4,3,2,1,0:T(8,128)(2,1)}, u32[]{:S(2)}) copy-start(bf16[3,3,3,16,384]{4,3,2,1,0:T(8,128)(2,1)} %param.10) | copy-start | bytes 995332
  2.9 22.9 %copy-start.15 = (f32[384]{0:T(512)S(1)}, f32[384]{0:T(512)}, u32[]{:S(2)}) copy-start(f32[384]{0:T(512)} %param.12) | copy-start | bytes 4612
  2.9 23.0 %copy-start.16 = (f32[384]{0:T(512)S(1)}, f32[384]{0:T(512)}, u32[]{:S(2)}) copy-start(f32[384]{0:T(512)} %param.11) | copy-start | bytes 4612
  19.5 6.5 %collective-permute-start.1 = (bf16[6,1,1664]{2,0,1:T(8,128)(2,1)S(1)}, bf16[6,1,1664]{2,0,1:T(8,128)(2,1)S(1)}, u32[]{:S(2)}, u32[]{:S(2)}) collective-permute-start(bf16[6,1,1664]{2,0,1:T(8,128)(2,1)S(1)} %fusion.19), channel_id=1, source_target_pairs={{2,0},{3,1},{6,4},{7,5},{10,8},{11,9},{14,12},{15,13},{18,16},{19,... | collective-permute-start | bytes 59912 | tf_op jit(solution)/shard_map/ppermute | solution.py:22
  20.8 6.1 %collective-permute-start = (bf16[6,1,1664]{2,0,1:T(8,128)(2,1)S(1)}, bf16[6,1,1664]{2,0,1:T(8,128)(2,1)S(1)}, u32[]{:S(2)}, u32[]{:S(2)}) collective-permute-start(bf16[6,1,1664]{2,0,1:T(8,128)(2,1)S(1)} %fusion.19), channel_id=1, source_target_pairs={{0,2},{1,3},{4,6},{5,7},{8,10},{9,11},{12,14},{13,15},{16,18},{17,... | collective-permute-start | bytes 59912 | tf_op jit(solution)/shard_map/ppermute | solution.py:20
  39.3 23.4 %collective-permute-start.3 = (bf16[4,1,104,192]{2,3,0,1:T(8,128)(2,1)}, bf16[4,1,104,192]{2,3,0,1:T(8,128)(2,1)}, u32[]{:S(2)}, u32[]{:S(2)}) collective-permute-start(bf16[4,1,104,192]{2,3,0,1:T(8,128)(2,1)} %select_bitcast_fusion), channel_id=1, source_target_pairs={{2,0},{3,1},{6,4},{7,5},{10,8},{11,9},{14,12},{15,13},{18,16},{19,... | collective-permute-start | bytes 479240 | tf_op jit(solution)/shard_map/ppermute | solution.py:22
  40.6 22.1 %collective-permute-start.2 = (bf16[4,1,104,192]{2,3,0,1:T(8,128)(2,1)}, bf16[4,1,104,192]{2,3,0,1:T(8,128)(2,1)}, u32[]{:S(2)}, u32[]{:S(2)}) collective-permute-start(bf16[4,1,104,192]{2,3,0,1:T(8,128)(2,1)} %select_bitcast_fusion), channel_id=1, source_target_pairs={{0,2},{1,3},{4,6},{5,7},{8,10},{9,11},{12,14},{13,15},{16,18},{17,... | collective-permute-start | bytes 479240 | tf_op jit(solution)/shard_map/ppermute | solution.py:20
  51.3 1.1 %copy-start.12 = (bf16[1,1,3,384,192]{3,4,2,1,0:T(8,128)(2,1)S(1)}, bf16[1,1,3,384,192]{3,4,2,1,0:T(8,128)(2,1)}, u32[]{:S(2)}) copy-start(bf16[1,1,3,384,192]{3,4,2,1,0:T(8,128)(2,1)} %get-tuple-element.21) | copy-start | bytes 1327108
  82.4 1.6 %copy-start.4 = (bf16[24,8,3,384]{3,1,2,0:T(8,128)(2,1)S(1)}, bf16[24,8,3,384]{3,1,2,0:T(8,128)(2,1)}, u32[]{:S(2)}) copy-start(bf16[24,8,3,384]{3,1,2,0:T(8,128)(2,1)} %copy.149) | copy-start | bytes 1327108
  82.5 1.9 %copy-start.5 = (bf16[24,8,3,384]{3,1,2,0:T(8,128)(2,1)S(1)}, bf16[24,8,3,384]{3,1,2,0:T(8,128)(2,1)}, u32[]{:S(2)}) copy-start(bf16[24,8,3,384]{3,1,2,0:T(8,128)(2,1)} %copy.150) | copy-start | bytes 1327108
  84.0 1.0 copy-start.6
  84.4 1.0 copy-start.7
  85.0 1.0 copy-start.8
  85.4 1.1 copy-start.1
  85.4 1.2 %copy-start.9 = (bf16[24,8,3,384]{3,1,2,0:T(8,128)(2,1)S(1)}, bf16[24,8,3,384]{3,1,2,0:T(8,128)(2,1)}, u32[]{:S(2)}) copy-start(bf16[24,8,3,384]{3,1,2,0:T(8,128)(2,1)} %copy.154) | copy-start | bytes 1327108
  86.1 1.1 copy-start.2
  86.1 1.2 %copy-start.10 = (bf16[24,8,3,384]{3,1,2,0:T(8,128)(2,1)S(1)}, bf16[24,8,3,384]{3,1,2,0:T(8,128)(2,1)}, u32[]{:S(2)}) copy-start(bf16[24,8,3,384]{3,1,2,0:T(8,128)(2,1)} %copy.155) | copy-start | bytes 1327108
  86.6 1.1 copy-start.3
  86.6 1.2 %copy-start.11 = (bf16[24,8,3,384]{3,1,2,0:T(8,128)(2,1)S(1)}, bf16[24,8,3,384]{3,1,2,0:T(8,128)(2,1)}, u32[]{:S(2)}) copy-start(bf16[24,8,3,384]{3,1,2,0:T(8,128)(2,1)} %copy.156) | copy-start | bytes 1327108
  87.8 6.6 %copy-start.13 = (f32[192]{0:T(256)S(1)}, f32[192]{0:T(256)}, u32[]{:S(2)}) copy-start(f32[192]{0:T(256)} %param.15) | copy-start | bytes 2308
  87.8 6.6 %copy-start.14 = (f32[192]{0:T(256)S(1)}, f32[192]{0:T(256)}, u32[]{:S(2)}) copy-start(f32[192]{0:T(256)} %param.14) | copy-start | bytes 2308
  95.5 7.0 %collective-permute-start.4 = (bf16[2,1,104,192]{2,0,3,1:T(2,128)(2,1)S(1)}, bf16[2,1,104,192]{2,0,3,1:T(2,128)(2,1)S(1)}, u32[]{:S(2)}, u32[]{:S(2)}) collective-permute-start(bf16[2,1,104,192]{2,0,3,1:T(2,128)(2,1)S(1)} %fusion.18), channel_id=1, source_target_pairs={{0,4},{4,8},{8,12},{12,0},{1,5},{5,9},{9,13},{13,1},{2,6},{6,10},{... | collective-permute-start | bytes 239624 | tf_op jit(solution)/shard_map/ppermute | solution.py:162
  97.3 6.8 %collective-permute-start.6 = (bf16[2,1,104,192]{2,0,3,1:T(2,128)(2,1)S(1)}, bf16[2,1,104,192]{2,0,3,1:T(2,128)(2,1)S(1)}, u32[]{:S(2)}, u32[]{:S(2)}) collective-permute-start(bf16[2,1,104,192]{2,0,3,1:T(2,128)(2,1)S(1)} %fusion.18), channel_id=1, source_target_pairs={{0,12},{4,0},{8,4},{12,8},{1,13},{5,1},{9,5},{13,9},{2,14},{6,2},{... | collective-permute-start | bytes 239624 | tf_op jit(solution)/shard_map/ppermute | solution.py:164
  102.6 6.4 %collective-permute-start.5 = (bf16[2,1,104,192]{2,0,3,1:T(2,128)(2,1)S(1)}, bf16[2,1,104,192]{2,0,3,1:T(2,128)(2,1)S(1)}, u32[]{:S(2)}, u32[]{:S(2)}) collective-permute-start(bf16[2,1,104,192]{2,0,3,1:T(2,128)(2,1)S(1)} %collective-permute-done.4), channel_id=1, source_target_pairs={{0,4},{4,8},{8,12},{12,0},{1,5},{5,9},{9,13},{13,1},{2,6},{6,10},{... | collective-permute-start | bytes 239624 | tf_op jit(solution)/shard_map/ppermute | solution.py:162
